TPU v7x, 32 devices: a whole 2x2x4 slice. The times are simulated.
32 devices in a mesh: dp: 8 (over z, x), mp: 4 (over y, core).
Axes of the slice: x: 2, y: 2, z: 4, core: 2. Of those that a mesh axis runs over, the one named last changes fastest.
Arguments:
- inputs: bfloat16 [16384, 768], P('dp'), may hold values from -6 to 6
- segments: int32 [256, 64], P('dp'), may hold values from 0 to 5, never falling along the last dimension, each value on 1 to 24 neighbouring positions
- cotangent: bfloat16 [16384, 768], P('dp'), may hold values from -12 to 12
- triple_weight: float32 [3, 768, 768], P(None, 'dp', 'mp'), may hold values from -0.21875 to 0.21875
- triple_first: float32 [3, 768, 768], P(None, 'dp', 'mp')
- triple_second: float32 [3, 768, 768], P(None, 'dp', 'mp'), as said below
- outward_weight: float32 [768, 768], P('mp', 'dp'), may hold values from -0.625 to 0.625
- outward_first: float32 [768, 768], P('mp', 'dp')
- outward_second: float32 [768, 768], P('mp', 'dp'), as said below
- expand_weight: float32 [768, 3072], P('dp', 'mp'), may hold values from -2 to 2
- expand_first: float32 [768, 3072], P('dp', 'mp')
- expand_second: float32 [768, 3072], P('dp', 'mp'), as said below
- reduce_weight: float32 [3072, 768], P('mp', 'dp'), may hold values from -0.109375 to 0.109375
- reduce_first: float32 [3072, 768], P('mp', 'dp')
- reduce_second: float32 [3072, 768], P('mp', 'dp'), as said below
- norm_params: float32 [6, 768], replicated, may hold values from -3 to 4
- norm_first: float32 [6, 768], replicated
- norm_second: float32 [6, 768], replicated, as said below
- paired_bias: float32 [2, 768], P(None, 'mp'), may hold values from -1.8 to 1.8
- paired_first: float32 [2, 768], P(None, 'mp')
- paired_second: float32 [2, 768], P(None, 'mp'), as said below
- hidden_bias: float32 [3072], P('mp'), may hold values from -1.8 to 1.8
- hidden_first: float32 [3072], P('mp')
- hidden_second: float32 [3072], P('mp'), as said below
Outputs:
- outputs: bfloat16 [16384, 768], P('dp')
- input_gradient: bfloat16 [16384, 768], P('dp')
- gradient_norm: float32 [], replicated
- triple_moment: float32 [3, 768, 768], P(None, 'dp', 'mp')
- triple_square: float32 [3, 768, 768], P(None, 'dp', 'mp')
- triple_updated: float32 [3, 768, 768], P(None, 'dp', 'mp')
- outward_moment: float32 [768, 768], P('mp', 'dp')
- outward_square: float32 [768, 768], P('mp', 'dp')
- outward_updated: float32 [768, 768], P('mp', 'dp')
- expand_moment: float32 [768, 3072], P('dp', 'mp')
- expand_square: float32 [768, 3072], P('dp', 'mp')
- expand_updated: float32 [768, 3072], P('dp', 'mp')
- reduce_moment: float32 [3072, 768], P('mp', 'dp')
- reduce_square: float32 [3072, 768], P('mp', 'dp')
- reduce_updated: float32 [3072, 768], P('mp', 'dp')
- norm_moment: float32 [6, 768], replicated
- norm_square: float32 [6, 768], replicated
- norm_updated: float32 [6, 768], replicated
- paired_moment: float32 [2, 768], P(None, 'mp')
- paired_square: float32 [2, 768], P(None, 'mp')
- paired_updated: float32 [2, 768], P(None, 'mp')
- hidden_moment: float32 [3072], P('mp')
- hidden_square: float32 [3072], P('mp')
- hidden_updated: float32 [3072], P('mp')
Inputs may be any that keep to these rules, and one draw needn't show every extreme that they name: `segments`: within each row of 64 tokens the numbers never fall; each of the 6 captions holds 1 to 24 tokens, one exactly 24. `triple_second`: positive. `outward_second`: positive. `expand_second`: positive. `reduce_second`: positive. `norm_second`: positive. `paired_second`: positive. `hidden_second`: positive.
All inputs are finite; a program needn't handle non-finite values.
Results may differ from a plain program's by a relative error of at most 0.02.
Values may be sent and summed in bfloat16 or wider, within the bound.
No kernel may reach another device: no remote copies, remote signals or barrier semaphores. Data moves between devices by JAX's collectives and lax.ppermute only.
A program may use at most 128 MiB of HBM per device.

v0:
```python
import jax
import jax.numpy as jnp
from jax import lax
from jax.sharding import PartitionSpec as P

HD = 64
STEP = 5
EPS_NORM = 1e-06
BETA = 0.5
LR_MATRIX = 0.03
LR_VECTOR = 0.2
DECAY = 0.1
ADAM_EPS = 1e-08
CLIP = 1.0
NEG = -1e30


def norm_forward(rows_in, gain_row, shift_row):
    row_mean = jnp.mean(rows_in, axis=-1, keepdims=True)
    centred = rows_in - row_mean
    variance = jnp.mean(centred * centred, axis=-1, keepdims=True)
    scaled = lax.rsqrt(variance + EPS_NORM)
    normal_rows = centred * scaled
    return (normal_rows * gain_row + shift_row, normal_rows, scaled)


def norm_backward(upstream, normal_rows, scaled, gain_row):
    gained = upstream * gain_row
    mean_one = jnp.mean(gained, axis=-1, keepdims=True)
    mean_two = jnp.mean(gained * normal_rows, axis=-1, keepdims=True)
    return scaled * (gained - mean_one - normal_rows * mean_two)


def smooth_gate(values_in):
    return jax.nn.gelu(values_in, approximate=True)


def adam_step(weight, first, second, grad, factor, rate, decay):
    clipped = grad * factor
    first_new = BETA * first + (1.0 - BETA) * clipped
    second_new = BETA * second + (1.0 - BETA) * clipped * clipped
    correction = 1.0 - BETA**STEP
    direction = first_new / correction / (jnp.sqrt(second_new / correction) + ADAM_EPS)
    return (first_new, second_new, weight - rate * (direction + decay * weight))


def per_device(
    inputs,
    segments,
    cotangent,
    triple_weight,
    triple_first,
    triple_second,
    outward_weight,
    outward_first,
    outward_second,
    expand_weight,
    expand_first,
    expand_second,
    reduce_weight,
    reduce_first,
    reduce_second,
    norm_params,
    norm_first,
    norm_second,
    paired_bias,
    paired_first,
    paired_second,
    hidden_bias,
    hidden_first,
    hidden_second,
):
    f32 = jnp.float32
    bf16 = jnp.bfloat16
    dp_count = lax.axis_size("dp")
    mp_count = lax.axis_size("mp")
    triple_full, outward_full, expand_full, reduce_full = (
        lax.all_gather(triple_weight.astype(bf16), "dp", axis=1, tiled=True),
        lax.all_gather(outward_weight.astype(bf16), "dp", axis=1, tiled=True),
        lax.all_gather(expand_weight.astype(bf16), "dp", axis=0, tiled=True),
        lax.all_gather(reduce_weight.astype(bf16), "dp", axis=1, tiled=True),
    )
    row_count, row_length = segments.shape
    token_count = inputs.shape[0]
    head_width = triple_full.shape[2]
    head_count = head_width // HD
    scale_factor = HD ** (-0.5)
    grid = (row_count, row_length, head_count, HD)
    x_full = inputs.astype(f32)
    normed_one, normal_one, scaled_one = norm_forward(x_full, norm_params[0], norm_params[1])
    first_low = normed_one.astype(bf16)
    projected = jnp.einsum("td,cdw->ctw", first_low, triple_full, preferred_element_type=f32)
    queries = (projected[0] + paired_bias[0]).astype(bf16).reshape(grid)
    key_rows = projected[1].astype(bf16).reshape(grid)
    value_rows = (projected[2] + paired_bias[1]).astype(bf16).reshape(grid)
    same_caption = (segments[:, :, None] == segments[:, None, :])[:, None, :, :]

    def scores_of(query_in, key_in):
        raw_scores = jnp.einsum("rqhd,rkhd->rhqk", query_in, key_in, preferred_element_type=f32)
        return jnp.where(same_caption, raw_scores * scale_factor, NEG)

    scores = scores_of(queries, key_rows)
    row_top = jnp.max(scores, axis=-1, keepdims=True)
    lifted = jnp.exp(scores - row_top)
    row_total = jnp.sum(lifted, axis=-1, keepdims=True)
    probs = lifted / row_total
    log_total = row_top + jnp.log(row_total)
    context = jnp.einsum(
        "rhqk,rkhd->rqhd", probs.astype(bf16), value_rows, preferred_element_type=f32
    )
    context_low = context.astype(bf16).reshape(token_count, head_width)
    attn_part = jnp.dot(context_low, outward_full, preferred_element_type=f32)
    attended = lax.psum(attn_part.astype(jnp.bfloat16), "mp").astype(jnp.float32)
    middle = x_full + attended + norm_params[4]
    normed_two, normal_two, scaled_two = norm_forward(middle, norm_params[2], norm_params[3])
    second_low = normed_two.astype(bf16)
    hidden_pre = jnp.dot(second_low, expand_full, preferred_element_type=f32) + hidden_bias
    gate_out, gelu_pull = jax.vjp(smooth_gate, hidden_pre)
    activated = gate_out.astype(bf16)
    fed_part = jnp.dot(activated, reduce_full, preferred_element_type=f32)
    fed = lax.psum(fed_part.astype(jnp.bfloat16), "mp").astype(jnp.float32)
    outputs = (middle + fed + norm_params[5]).astype(bf16)
    cot_full = cotangent.astype(f32)
    grad_reduce = jnp.einsum("tf,td->fd", activated, cotangent, preferred_element_type=f32)
    act_grad = jnp.einsum("td,fd->tf", cotangent, reduce_full, preferred_element_type=f32)
    hidden_grad = gelu_pull(act_grad)[0].astype(bf16)
    grad_expand = jnp.einsum("td,tf->df", second_low, hidden_grad, preferred_element_type=f32)
    grad_hidden = jnp.sum(hidden_grad, axis=0, dtype=f32)
    second_part = jnp.einsum("tf,df->td", hidden_grad, expand_full, preferred_element_type=f32)
    second_grad = lax.psum(second_part.astype(jnp.bfloat16), "mp").astype(jnp.float32)
    middle_grad = cot_full + norm_backward(second_grad, normal_two, scaled_two, norm_params[2])
    middle_low = middle_grad.astype(bf16)
    grad_outward = jnp.einsum("tw,td->wd", context_low, middle_low, preferred_element_type=f32)
    context_grad = (
        jnp.einsum("td,wd->tw", middle_low, outward_full, preferred_element_type=f32)
        .astype(bf16)
        .reshape(grid)
    )
    probs_again = jnp.exp(scores_of(queries, key_rows) - log_total)
    probs_low = probs_again.astype(bf16)
    value_grad = jnp.einsum(
        "rhqk,rqhd->rkhd", probs_low, context_grad, preferred_element_type=f32
    ).astype(bf16)
    prob_grad = jnp.einsum("rqhd,rkhd->rhqk", context_grad, value_rows, preferred_element_type=f32)
    inner = jnp.sum(prob_grad * probs_again, axis=-1, keepdims=True)
    score_grad = (probs_again * (prob_grad - inner) * scale_factor).astype(bf16)
    query_grad = jnp.einsum(
        "rhqk,rkhd->rqhd", score_grad, key_rows, preferred_element_type=f32
    ).astype(bf16)
    key_grad = jnp.einsum(
        "rhqk,rqhd->rkhd", score_grad, queries, preferred_element_type=f32
    ).astype(bf16)
    stacked = jnp.stack([query_grad, key_grad, value_grad]).reshape(3, token_count, head_width)
    grad_triple = jnp.einsum("td,ctw->cdw", first_low, stacked, preferred_element_type=f32)
    grad_paired = jnp.stack(
        [jnp.sum(stacked[0], axis=0, dtype=f32), jnp.sum(stacked[2], axis=0, dtype=f32)]
    )
    first_part = jnp.einsum("ctw,cdw->td", stacked, triple_full, preferred_element_type=f32)
    first_grad = lax.psum(first_part.astype(jnp.bfloat16), "mp").astype(jnp.float32)
    input_gradient = (
        middle_grad + norm_backward(first_grad, normal_one, scaled_one, norm_params[0])
    ).astype(bf16)
    grad_norms = jnp.stack(
        [
            jnp.sum(first_grad * normal_one, axis=0),
            jnp.sum(first_grad, axis=0),
            jnp.sum(second_grad * normal_two, axis=0),
            jnp.sum(second_grad, axis=0),
            jnp.sum(middle_grad, axis=0),
            jnp.sum(cot_full, axis=0),
        ]
    )
    owned = (
        lax.psum_scatter(grad_triple, "dp", scatter_dimension=1, tiled=True),
        lax.psum_scatter(grad_outward, "dp", scatter_dimension=1, tiled=True),
        lax.psum_scatter(grad_expand, "dp", scatter_dimension=0, tiled=True),
        lax.psum_scatter(grad_reduce, "dp", scatter_dimension=1, tiled=True),
    )
    vectors = lax.psum((grad_norms, grad_paired, grad_hidden), "dp")
    local_square = jnp.zeros((), f32)
    for grad_item in owned:
        local_square = local_square + jnp.sum(grad_item * grad_item)
    local_square = local_square + jnp.sum(vectors[0] * vectors[0]) / (dp_count * mp_count)
    local_square = (
        local_square
        + (jnp.sum(vectors[1] * vectors[1]) + jnp.sum(vectors[2] * vectors[2])) / dp_count
    )
    total_square = lax.psum(local_square, ("dp", "mp"))
    gradient_norm = jnp.sqrt(total_square)
    factor = jnp.minimum(1.0, CLIP / gradient_norm)
    triple_new = adam_step(
        triple_weight, triple_first, triple_second, owned[0], factor, LR_MATRIX, DECAY
    )
    outward_new = adam_step(
        outward_weight, outward_first, outward_second, owned[1], factor, LR_MATRIX, DECAY
    )
    expand_new = adam_step(
        expand_weight, expand_first, expand_second, owned[2], factor, LR_MATRIX, DECAY
    )
    reduce_new = adam_step(
        reduce_weight, reduce_first, reduce_second, owned[3], factor, LR_MATRIX, DECAY
    )
    norm_new = adam_step(norm_params, norm_first, norm_second, vectors[0], factor, LR_VECTOR, 0.0)
    paired_new = adam_step(
        paired_bias, paired_first, paired_second, vectors[1], factor, LR_VECTOR, 0.0
    )
    hidden_new = adam_step(
        hidden_bias, hidden_first, hidden_second, vectors[2], factor, LR_VECTOR, 0.0
    )
    return (
        outputs,
        input_gradient,
        gradient_norm,
        triple_new[0],
        triple_new[1],
        triple_new[2],
        outward_new[0],
        outward_new[1],
        outward_new[2],
        expand_new[0],
        expand_new[1],
        expand_new[2],
        reduce_new[0],
        reduce_new[1],
        reduce_new[2],
        norm_new[0],
        norm_new[1],
        norm_new[2],
        paired_new[0],
        paired_new[1],
        paired_new[2],
        hidden_new[0],
        hidden_new[1],
        hidden_new[2],
    )


def solution(mesh):
    placed = (
        P("dp", None),
        P("dp", None),
        P("dp", None),
        P(None, "dp", "mp"),
        P(None, "dp", "mp"),
        P(None, "dp", "mp"),
        P("mp", "dp"),
        P("mp", "dp"),
        P("mp", "dp"),
        P("dp", "mp"),
        P("dp", "mp"),
        P("dp", "mp"),
        P("mp", "dp"),
        P("mp", "dp"),
        P("mp", "dp"),
        P(),
        P(),
        P(),
        P(None, "mp"),
        P(None, "mp"),
        P(None, "mp"),
        P("mp"),
        P("mp"),
        P("mp"),
    )
    return jax.shard_map(
        per_device,
        mesh=mesh,
        in_specs=placed,
        out_specs=(
            P("dp", None),
            P("dp", None),
            P(),
            P(None, "dp", "mp"),
            P(None, "dp", "mp"),
            P(None, "dp", "mp"),
            P("mp", "dp"),
            P("mp", "dp"),
            P("mp", "dp"),
            P("dp", "mp"),
            P("dp", "mp"),
            P("dp", "mp"),
            P("mp", "dp"),
            P("mp", "dp"),
            P("mp", "dp"),
            P(),
            P(),
            P(),
            P(None, "mp"),
            P(None, "mp"),
            P(None, "mp"),
            P("mp"),
            P("mp"),
            P("mp"),
        ),
        check_vma=False,
    )
```

profile of v0, /device:TPU:0, one launch (start us, length us, event | category | flops | bytes accessed | tf_op | source)
XLA Modules:
  0.0 715.4 jit_solution(5087993690982692376)
XLA Ops:
  8.1 2.5 convert_reduce_fusion.2
  12.8 40.5 %all_gather.12 = bf16[3,768,192]{2,0,1:T(4,128)(2,1)} all-gather(bf16[3,96,192]{2,0,1:T(4,128)(2,1)S(1)} %copy.118), channel_id=1, replica_groups=mesh['dp'=8,'mp'=4] {'dp'}, dimensions={1}, use_global_device_ids=true | all-gather | bytes 995328 | tf_op jit(solution)/shard_map/all_gather | solution.py:78
  53.2 3.4 copy.119
  56.7 3.4 fusion.96
  61.1 2.0 fusion.107
  65.1 31.9 %all_gather.13 = bf16[192,768]{0,1:T(8,128)(2,1)S(1)} all-gather(bf16[192,96]{0,1:T(8,128)(2,1)} %copy.127), channel_id=1, replica_groups=mesh['dp'=8,'mp'=4] {'dp'}, dimensions={1}, use_global_device_ids=true | all-gather | bytes 331776 | tf_op jit(solution)/shard_map/all_gather | solution.py:79
  97.0 3.4 convert_element_type.130
  100.4 3.4 copy.123
  103.8 3.6 squeeze.4
  107.4 3.9 copy.120
  111.3 3.6 squeeze.10
  114.9 5.7 fusion.108
  121.5 2.1 copy-done.5
  124.7 2.2 copy.126
  126.9 3.5 reshape.145
  130.4 3.9 convolution_convert_fusion.2
  138.0 63.8 %all-reduce.6.cloned.1.call-done = bf16[2048,768]{1,0:T(8,128)(2,1)} async-done(((bf16[2048,768]{1,0:T(8,128)(2,1)}), bf16[2048,768]{1,0:T(8,128)(2,1)}) %all-reduce.6.cloned.1.call-update) | async-done | bytes 3145744 | tf_op jit(solution)/shard_map/psum | solution.py:113
  201.8 3.1 fusion.46
  205.0 1.8 multiply_reduce_fusion
  207.4 3.0 add_convert_fusion.1
  210.4 7.5 %fusion.111 = f32[2048,768]{1,0:T(8,128)} fusion(bf16[2048,768]{1,0:T(8,128)(2,1)} %add_convert_fusion.1, bf16[768,768]{1,0:T(8,128)(2,1)} %all-gather.3.cloned.1.call-done), kind=kOutput, calls=%fused_computation.161 | convolution fusion | flops 2415919104 | bytes 10616832 | tf_op jit(solution)/shard_map/dot_general | solution.py:117
  217.9 2.4 all-gather.5.cloned.1.call-done
  220.3 10.8 %convert_reduce_fusion.4 = (f32[768]{0:T(1024)}, bf16[2048,768]{1,0:T(8,128)(2,1)S(1)}, bf16[2048,768]{1,0:T(8,128)(2,1)}) fusion(f32[2048,768]{1,0:T(8,128)} %fusion.111, f32[768]{0:T(1024)} %param.45, bf16[2048,768]{1,0:T(8,128)(2,1)} %param.26, bf16[768,768]{0,1:T(8,128)(2,1)} %all-gather.5.cloned.1.call-done), kind=kOutput, calls=%fused_computation.46 | convolution fusion | flops 2455239936 | bytes 16914432 | tf_op jit(solution)/shard_map/td,fd->tf/dot_general | solution.py:125
  231.1 1.7 copy-done.57
  232.8 4.0 convolution_convert_fusion
  238.7 6.6 convolution_convert_fusion.1
  245.2 58.7 %all-reduce.8.cloned.1.call-done = bf16[2048,768]{1,0:T(8,128)(2,1)} async-done(((bf16[2048,768]{1,0:T(8,128)(2,1)}), bf16[2048,768]{1,0:T(8,128)(2,1)}) %all-reduce.8.cloned.1.call-update) | async-done | bytes 3145744 | tf_op jit(solution)/shard_map/psum | solution.py:130
  303.9 7.1 fusion.30
  311.1 4.7 fusion.106
  315.8 2.7 copy-done.3
  318.5 2.3 fusion.78
  320.7 4.9 convolution_convert_fusion.3
  325.6 3.4 reshape.146
  329.0 3.6 copy.128
  332.7 5.1 fusion.81
  337.8 10.3 %fusion.71 = bf16[32,64,3,64]{1,3,2,0:T(8,128)(2,1)} fusion(f32[32,3,64,64]{2,3,1,0:T(8,128)} %fusion.81, f32[32,3,64,64]{2,3,1,0:T(8,128)} %copy-done.4, f32[32,3,64]{2,1,0:T(4,128)S(1)} %copy-done.23, f32[32,64,3,64]{1,0,3,2:T(8,128)} %squeeze.10, f32[3,64]{1,0:T(4,128)S(1)} %copy-done.47), kind=kOutput, calls=%fused_computation.91 | convolution fusion | flops 54270016 | bytes 5530368 | tf_op jit(solution)/shard_map/rhqk,rqhd->rkhd/dot_general | solution.py:150
  348.1 8.1 %convert_reduce_fusion.6 = (f32[3,64]{1,0:T(4,128)S(1)}, bf16[32,64,3,64]{3,1,2,0:T(8,128)(2,1)}) fusion(bf16[32,64,3,64]{3,1,2,0:T(8,128)(2,1)} %copy.123, f32[32,3,64,64]{2,3,1,0:T(8,128)} %fusion.81, f32[32,3,64,64]{2,3,1,0:T(8,128)} %copy-done.4, f32[32,3,64]{2,1,0:T(4,128)S(1)} %copy-done.23), kind=kOutput, calls=%fused_computation.60 | convolution fusion | flops 54269824 | bytes 4743936 | tf_op jit(solution)/shard_map/rhqk,rkhd->rqhd/dot_general | solution.py:147
  356.2 4.4 convert_reduce_fusion.5
  360.6 3.6 copy.131
  364.2 3.5 stack.42
  367.8 2.1 constant_dynamic-update-slice_fusion.2
  369.9 3.6 copy.133
  373.4 3.5 stack.43
  377.0 3.2 copy.135
  380.1 3.5 stack.44
  383.7 2.2 constant_dynamic-update-slice_fusion.1
  385.8 2.1 constant_dynamic-update-slice_fusion
  387.9 6.0 bitcast_convert_fusion
  394.0 7.1 fusion.112
  401.4 6.9 fusion.113
  408.4 5.2 fusion.65
  413.6 4.2 copy.149
  417.8 4.7 reshape.151
  423.4 1.8 copy.137
  425.3 1.8 copy.138
  429.0 85.0 %all-reduce.10.cloned.1.call-done = (bf16[2048,768]{1,0:T(8,128)(2,1)}, bf16[2048,768]{1,0:T(8,128)(2,1)}) async-done(((bf16[2048,768]{1,0:T(8,128)(2,1)}, bf16[2048,768]{1,0:T(8,128)(2,1)}), (bf16[2048,768]{1,0:T(8,128)(2,1)}, bf16[2048,768]{1,0:T(8,128)(2,1)})) %all-reduce.10.cloned.1.call-update) | async-done | bytes 6291472 | tf_op jit(solution)/shard_map/psum | solution.py:121
  514.0 4.6 fusion.31
  518.7 37.3 %all-reduce = (f32[6,768]{1,0:T(8,128)S(1)}, f32[2,192]{1,0:T(2,128)S(1)}, f32[768]{0:T(1024)S(1)}) all-reduce(f32[6,768]{1,0:T(8,128)S(1)} %stack.52, f32[2,192]{1,0:T(2,128)S(1)} %pad_maximum_fusion, f32[768]{0:T(1024)S(1)} %copy-done.53), channel_id=1, replica_groups=mesh['dp'=8,'mp'=4] {'dp'}, use_global_device_ids=true, to_apply=%region_29.30 | all-reduce | flops 5760 | bytes 46080 | tf_op jit(solution)/shard_map/psum | solution.py:179
  559.8 1.6 multiply_reduce_fusion.3
  561.4 6.3 reduce-scatter.11.cloned.1.call-done
  570.5 67.2 %reduce-scatter.13.cloned.1.call-done = f32[96,576]{1,0:T(8,128)} async-done(((f32[768,576]{1,0:T(8,128)}), f32[96,576]{1,0:T(8,128)}) %reduce-scatter.13.cloned.1.call-update) | async-done | bytes 221200
  637.7 1.9 reshape.152
  644.0 10.6 %fusion.16 = (bf16[2048,768]{1,0:T(8,128)(2,1)}, bf16[2048,768]{1,0:T(8,128)(2,1)}) fusion(f32[2048,768]{1,0:T(8,128)} %copy-done.3, bf16[2048,768]{1,0:T(8,128)(2,1)S(1)} %copy-done, bf16[2048,768]{1,0:T(8,128)(2,1)} %get-tuple-element.140, f32[2048]{0:T(1024)} %broadcast_multiply_fusion, f32[2048]{0:T(1024)} %broadcast_multiply_fusion.1, ...), kind=kLoop, calls=%fused_computation.29 | loop fusion | flops 28311552 | bytes 25207808 | tf_op jit(solution)/shard_map/convert_element_type | solution.py:162
  654.7 39.5 %psum.63 = f32[]{:T(128)} all-reduce(f32[]{:T(128)S(6)} %add.294), channel_id=1, replica_groups=mesh['dp'=8,'mp'=4] {'dp','mp'}, use_global_device_ids=true, to_apply=%region_38.39 | all-reduce | flops 1 | bytes 8 | tf_op jit(solution)/shard_map/psum | solution.py:188
  (185 shorter events, 34.8 us)
Async XLA Ops:
  8.0 2.8 copy-start
  8.0 3.9 copy-start.31
  8.0 4.5 copy-start.13
  8.1 193.7 %all-reduce.6.cloned.1.call-start = ((), (), s32[]{:S(2)}) async-start(), calls=%async_computation.4 | async-start | bytes 6291456 | tf_op jit(solution)/shard_map/psum | solution.py:113
  10.9 45.8 %copy-start.25 = (f32[2048]{0:T(1024)}, f32[2048]{0:T(1024)S(1)}, u32[]{:S(2)}) copy-start(f32[2048]{0:T(1024)S(1)} %broadcast_multiply_fusion.5) | copy-start | bytes 24580
  12.0 48.1 %copy-start.32 = (f32[2048]{0:T(1024)}, f32[2048]{0:T(1024)S(1)}, u32[]{:S(2)}) copy-start(f32[2048]{0:T(1024)S(1)} %add_rsqrt_fusion.1) | copy-start | bytes 24580
  12.6 47.5 %copy-start.35 = (f32[768]{0:T(1024)}, f32[768]{0:T(1024)S(1)}, u32[]{:S(2)}) copy-start(f32[768]{0:T(1024)S(1)} %get-tuple-element.133) | copy-start | bytes 9220
  12.6 47.5 %copy-start.54 = (f32[768]{0:T(1024)}, f32[768]{0:T(1024)S(1)}, u32[]{:S(2)}) copy-start(f32[768]{0:T(1024)S(1)} %get-tuple-element.132) | copy-start | bytes 9220
  61.1 2.0 copy-start.50
  61.1 2.2 copy-start.17
  61.1 2.9 copy-start.34
  63.2 58.3 %copy-start.44 = (f32[3,64]{1,0:T(4,128)}, f32[3,64]{1,0:T(4,128)S(1)}, u32[]{:S(2)}) copy-start(f32[3,64]{1,0:T(4,128)S(1)} %add.264) | copy-start | bytes 2308
  63.3 51.6 %copy-start.46 = (f32[3,64]{1,0:T(4,128)}, f32[3,64]{1,0:T(4,128)S(1)}, u32[]{:S(2)}) copy-start(f32[3,64]{1,0:T(4,128)S(1)} %add.267) | copy-start | bytes 2308
  120.6 4.1 copy-start.4
  120.6 4.1 copy-start.16
  120.6 3.0 copy-start.5
  134.3 76.0 %all-gather.3.cloned.1.call-start = ((), (), s32[]{:S(2)}) async-start(), calls=%async_computation.5 | async-start | bytes 1327104 | tf_op jit(solution)/shard_map/all_gather | solution.py:80
  136.0 84.2 %all-gather.5.cloned.1.call-start = ((), (), s32[]{:S(2)}) async-start(), calls=%async_computation.6 | async-start | bytes 1327104 | tf_op jit(solution)/shard_map/all_gather | solution.py:81
  137.8 166.2 %all-reduce.8.cloned.1.call-start = ((), (), s32[]{:S(2)}) async-start(), calls=%async_computation.7 | async-start | bytes 6291456 | tf_op jit(solution)/shard_map/psum | solution.py:130
  201.8 3.2 copy-start.1
  205.0 2.4 copy-start.37
  220.3 12.5 %copy-start.56 = (bf16[768,768]{1,0:T(8,128)(2,1)S(1)}, bf16[768,768]{1,0:T(8,128)(2,1)}, u32[]{:S(2)}) copy-start(bf16[768,768]{1,0:T(8,128)(2,1)} %all-gather.3.cloned.1.call-done) | copy-start | bytes 3538948
  236.9 190.5 %reduce-scatter.15.cloned.1.call-start = ((), (), s32[]{:S(2)}) async-start(), calls=%async_computation.11 | async-start | bytes 884736
  303.9 7.1 copy-start.2
  303.9 7.1 copy-start.6
  303.9 7.1 copy-start.8
  303.9 7.1 copy-start.28
  311.0 7.4 %copy-start.7 = (bf16[2048,192]{0,1:T(8,128)(2,1)S(1)}, bf16[2048,192]{0,1:T(8,128)(2,1)}, u32[]{:S(2)}) copy-start(bf16[2048,192]{0,1:T(8,128)(2,1)} %reshape.145) | copy-start | bytes 2359300
  315.8 2.7 copy-start.3
  325.6 7.0 copy-start.45
  332.6 5.1 copy-start.23
  332.6 5.1 copy-start.47
  360.5 153.4 %all-reduce.10.cloned.1.call-start = ((), (), s32[]{:S(2)}) async-start(), calls=%async_computation.12 | async-start | bytes 12582912 | tf_op jit(solution)/shard_map/psum | solution.py:121
  383.7 4.3 copy-start.15
  394.0 165.8 %reduce-scatter.9.cloned.1.call-start = ((), (), s32[]{:S(2)}) async-start(), calls=%async_computation.8 | async-start | bytes 2654208 | tf_op jit(solution)/shard_map/reduce_scatter | solution.py:176
  401.1 7.3 %copy-start.26 = (f32[2048]{0:T(1024)S(1)}, f32[2048]{0:T(1024)}, u32[]{:S(2)}) copy-start(f32[2048]{0:T(1024)} %copy-done.25) | copy-start | bytes 24580
  401.1 7.3 %copy-start.33 = (f32[2048]{0:T(1024)S(1)}, f32[2048]{0:T(1024)}, u32[]{:S(2)}) copy-start(f32[2048]{0:T(1024)} %copy-done.32) | copy-start | bytes 24580
  401.1 7.3 %copy-start.36 = (f32[768]{0:T(1024)S(1)}, f32[768]{0:T(1024)}, u32[]{:S(2)}) copy-start(f32[768]{0:T(1024)} %copy-done.35) | copy-start | bytes 9220
  401.1 7.3 %copy-start.55 = (f32[768]{0:T(1024)S(1)}, f32[768]{0:T(1024)}, u32[]{:S(2)}) copy-start(f32[768]{0:T(1024)} %copy-done.54) | copy-start | bytes 9220
  401.1 166.6 %reduce-scatter.11.cloned.1.call-start = ((), (), s32[]{:S(2)}) async-start(), calls=%async_computation.9 | async-start | bytes 2654208 | tf_op jit(solution)/shard_map/reduce_scatter | solution.py:177
  408.3 229.4 %reduce-scatter.13.cloned.1.call-start = ((), (), s32[]{:S(2)}) async-start(), calls=%async_computation.10 | async-start | bytes 2211840
  417.8 4.8 copy-start.14
  422.5 4.6 copy-start.39
  422.5 4.6 copy-start.38
  422.5 4.6 copy-start.43
  422.5 4.6 copy-start.42
  514.0 4.7 copy-start.53
  556.0 83.6 %copy-start.30 = (f32[6,768]{1,0:T(8,128)}, f32[6,768]{1,0:T(8,128)S(1)}, u32[]{:S(2)}) copy-start(f32[6,768]{1,0:T(8,128)S(1)} %get-tuple-element.136) | copy-start | bytes 55300
  556.0 83.6 %copy-start.40 = (f32[768]{0:T(1024)}, f32[768]{0:T(1024)S(1)}, u32[]{:S(2)}) copy-start(f32[768]{0:T(1024)S(1)} %get-tuple-element.138) | copy-start | bytes 9220
  556.0 83.6 %copy-start.48 = (f32[2,192]{1,0:T(2,128)}, f32[2,192]{1,0:T(2,128)S(1)}, u32[]{:S(2)}) copy-start(f32[2,192]{1,0:T(2,128)S(1)} %get-tuple-element.137) | copy-start | bytes 4612
  654.6 44.5 %copy-start.49 = (f32[2,192]{1,0:T(2,128)S(1)}, f32[2,192]{1,0:T(2,128)}, u32[]{:S(2)}) copy-start(f32[2,192]{1,0:T(2,128)} %copy-done.48) | copy-start | bytes 4612
  654.6 44.5 %copy-start.51 = (f32[2,192]{1,0:T(2,128)S(1)}, f32[2,192]{1,0:T(2,128)}, u32[]{:S(2)}) copy-start(f32[2,192]{1,0:T(2,128)} %param.42) | copy-start | bytes 4612
  654.6 45.8 %copy-start.41 = (f32[768]{0:T(1024)S(1)}, f32[768]{0:T(1024)}, u32[]{:S(2)}) copy-start(f32[768]{0:T(1024)} %copy-done.40) | copy-start | bytes 9220
  654.6 45.8 %copy-start.52 = (f32[768]{0:T(1024)S(1)}, f32[768]{0:T(1024)}, u32[]{:S(2)}) copy-start(f32[768]{0:T(1024)} %param.45) | copy-start | bytes 9220
  654.7 48.5 %copy-start.18 = (f32[192,96]{1,0:T(8,128)S(1)}, f32[192,96]{1,0:T(8,128)}, u32[]{:S(2)}) copy-start(f32[192,96]{1,0:T(8,128)} %param.30) | copy-start | bytes 221188
  654.7 48.5 %copy-start.29 = (f32[192,96]{1,0:T(8,128)S(1)}, f32[192,96]{1,0:T(8,128)}, u32[]{:S(2)}) copy-start(f32[192,96]{1,0:T(8,128)} %param.32) | copy-start | bytes 221188
  654.7 50.1 %copy-start.9 = (f32[96,768]{1,0:T(8,128)S(1)}, f32[96,768]{1,0:T(8,128)}, u32[]{:S(2)}) copy-start(f32[96,768]{1,0:T(8,128)} %param.33) | copy-start | bytes 884740
  654.7 50.1 %copy-start.11 = (f32[96,768]{1,0:T(8,128)S(1)}, f32[96,768]{1,0:T(8,128)}, u32[]{:S(2)}) copy-start(f32[96,768]{1,0:T(8,128)} %reduce-scatter.9.cloned.1.call-done) | copy-start | bytes 884740
  654.7 50.1 %copy-start.19 = (f32[96,768]{1,0:T(8,128)S(1)}, f32[96,768]{1,0:T(8,128)}, u32[]{:S(2)}) copy-start(f32[96,768]{1,0:T(8,128)} %param.35) | copy-start | bytes 884740
  654.7 50.1 %copy-start.20 = (f32[96,768]{1,0:T(8,128)S(1)}, f32[96,768]{1,0:T(8,128)}, u32[]{:S(2)}) copy-start(f32[96,768]{1,0:T(8,128)} %param.34) | copy-start | bytes 884740
  695.0 10.9 %copy-start.10 = (f32[768,96]{0,1:T(8,128)S(1)}, f32[768,96]{0,1:T(8,128)}, u32[]{:S(2)}) copy-start(f32[768,96]{0,1:T(8,128)} %param.36) | copy-start | bytes 884740
  695.0 10.9 %copy-start.12 = (f32[768,96]{0,1:T(8,128)S(1)}, f32[768,96]{0,1:T(8,128)}, u32[]{:S(2)}) copy-start(f32[768,96]{0,1:T(8,128)} %reduce-scatter.11.cloned.1.call-done) | copy-start | bytes 884740
  695.0 10.9 %copy-start.21 = (f32[768,96]{0,1:T(8,128)S(1)}, f32[768,96]{0,1:T(8,128)}, u32[]{:S(2)}) copy-start(f32[768,96]{0,1:T(8,128)} %param.38) | copy-start | bytes 884740
  696.5 9.4 %copy-start.22 = (f32[768,96]{0,1:T(8,128)S(1)}, f32[768,96]{0,1:T(8,128)}, u32[]{:S(2)}) copy-start(f32[768,96]{0,1:T(8,128)} %param.37) | copy-start | bytes 884740
  (3 other events, 3.3 us)
Sparse Core Ops, SparseCore 0:
  134.4 67.2 all-reduce.5
  237.0 66.9 all-reduce.7
  394.1 119.8 all-reduce.9
Sparse Core Ops, SparseCore 1:
  137.6 40.2 all-gather.2
  180.5 39.8 all-gather.4
  360.6 62.6 reduce-scatter.14
  427.2 68.3 reduce-scatter.8
  499.5 68.2 reduce-scatter.10
  571.6 66.1 reduce-scatter.12
where the time goes:
time: 722 us; the launch traced here: 715 us
  waiting for transfers between devices  284 us (39%)
  blocking collectives  149 us (21%)
  matrix products  103 us (14%)
  local copies, waits for them, and re-layouts  94 us (13%)
  other arithmetic  62.2 us (9%)
  between operations  22.6 us (3%)
    psum x1, waiting for transfers between devices, per_device(): fed = lax.psum(fed_part.astype(jnp.bfloat16), 'mp').astype(jnp.float32)  85 us
    unnamed x11, waiting for transfers between devices  67.4 us
    psum x1, waiting for transfers between devices, per_device(): lax.psum(attn_part.astype(jnp.bfloat16), 'mp').astype(jnp.float32)  63.8 us
    psum x1, waiting for transfers between devices, per_device(): lax.psum(second_part.astype(jnp.bfloat16), 'mp').astype(jnp.float32)  58.7 us
    all_gather x1, blocking collectives, per_device(): lax.all_gather(triple_weight.astype(bf16), 'dp', axis=1, tiled=True)  40.5 us
    psum x1, blocking collectives, per_device(): total_square = lax.psum(local_square, ('dp', 'mp'))  39.5 us
    psum x1, blocking collectives, per_device(): vectors = lax.psum((grad_norms, grad_paired, grad_hidden), 'dp')  37.3 us
    unnamed x130, local copies, waits for them, and re-layouts  32.6 us
  transfers between devices with their start and end apart: 9, of which 6 were waited for; matrix products, arithmetic and copies ran while one was open for 15% of the time, Pallas kernels for 0%

commit v1 on v0

--- a/solution.py
+++ b/solution.py
@@ -185,7 +185,7 @@
         local_square
         + (jnp.sum(vectors[1] * vectors[1]) + jnp.sum(vectors[2] * vectors[2])) / dp_count
     )
-    total_square = lax.psum(local_square, ("dp", "mp"))
+    total_square = lax.psum(lax.psum(local_square, "mp"), "dp")
     gradient_norm = jnp.sqrt(total_square)
     factor = jnp.minimum(1.0, CLIP / gradient_norm)
     triple_new = adam_step(

time: 722 us -> 709 us (0.982)
  blocking collectives: 149 us -> 136 us
    psum x1 -> x2, blocking collectives: 39.5 us -> 25.8 us  [per_device(): total_square = lax.psum(lax.psum(local_square, 'mp'), 'dp')]
where the time goes in v1:
time: 709 us; the launch traced here: 703 us
  waiting for transfers between devices  283 us (40%)
  blocking collectives  136 us (19%)
  matrix products  103 us (15%)
  local copies, waits for them, and re-layouts  94 us (13%)
  other arithmetic  63.4 us (9%)
  between operations  22.5 us (3%)
    psum x1, waiting for transfers between devices, per_device(): fed = lax.psum(fed_part.astype(jnp.bfloat16), 'mp').astype(jnp.float32)  85 us
    unnamed x11, waiting for transfers between devices  68 us
    psum x1, waiting for transfers between devices, per_device(): lax.psum(attn_part.astype(jnp.bfloat16), 'mp').astype(jnp.float32)  63.8 us
    psum x1, waiting for transfers between devices, per_device(): lax.psum(second_part.astype(jnp.bfloat16), 'mp').astype(jnp.float32)  58.7 us
    all_gather x1, blocking collectives, per_device(): lax.all_gather(triple_weight.astype(bf16), 'dp', axis=1, tiled=True)  40.5 us
    psum x1, blocking collectives, per_device(): vectors = lax.psum((grad_norms, grad_paired, grad_hidden), 'dp')  37.8 us
    unnamed x130, local copies, waits for them, and re-layouts  32.6 us
    all_gather x1, blocking collectives, per_device(): lax.all_gather(outward_weight.astype(bf16), 'dp', axis=1, tiled=True)  31.9 us
  transfers between devices with their start and end apart: 9, of which 6 were waited for; matrix products, arithmetic and copies ran while one was open for 15% of the time, Pallas kernels for 0%

profile of v1, /device:TPU:0, one launch (start us, length us, event | category | flops | bytes accessed | tf_op | source)
XLA Modules:
  0.0 702.9 jit_solution(3905411026837981229)
XLA Ops:
  8.1 2.5 convert_reduce_fusion.2
  12.8 40.5 %all_gather.12 = bf16[3,768,192]{2,0,1:T(4,128)(2,1)} all-gather(bf16[3,96,192]{2,0,1:T(4,128)(2,1)S(1)} %copy.118), channel_id=1, replica_groups=mesh['dp'=8,'mp'=4] {'dp'}, dimensions={1}, use_global_device_ids=true | all-gather | bytes 995328 | tf_op jit(solution)/shard_map/all_gather | solution.py:78
  53.2 3.4 copy.119
  56.7 3.4 fusion.96
  61.1 2.0 fusion.107
  65.1 31.9 %all_gather.13 = bf16[192,768]{0,1:T(8,128)(2,1)S(1)} all-gather(bf16[192,96]{0,1:T(8,128)(2,1)} %copy.127), channel_id=1, replica_groups=mesh['dp'=8,'mp'=4] {'dp'}, dimensions={1}, use_global_device_ids=true | all-gather | bytes 331776 | tf_op jit(solution)/shard_map/all_gather | solution.py:79
  97.0 3.4 convert_element_type.130
  100.4 3.4 copy.123
  103.8 3.6 squeeze.4
  107.4 3.9 copy.120
  111.3 3.6 squeeze.10
  114.9 5.7 fusion.108
  121.5 2.1 copy-done.5
  124.7 2.2 copy.126
  126.9 3.5 reshape.145
  130.4 3.9 convolution_convert_fusion.2
  138.0 63.8 %all-reduce.6.cloned.1.call-done = bf16[2048,768]{1,0:T(8,128)(2,1)} async-done(((bf16[2048,768]{1,0:T(8,128)(2,1)}), bf16[2048,768]{1,0:T(8,128)(2,1)}) %all-reduce.6.cloned.1.call-update) | async-done | bytes 3145744 | tf_op jit(solution)/shard_map/psum | solution.py:113
  201.8 3.1 fusion.46
  205.0 1.8 multiply_reduce_fusion
  207.4 3.0 add_convert_fusion.1
  210.4 7.5 %fusion.111 = f32[2048,768]{1,0:T(8,128)} fusion(bf16[2048,768]{1,0:T(8,128)(2,1)} %add_convert_fusion.1, bf16[768,768]{1,0:T(8,128)(2,1)} %all-gather.3.cloned.1.call-done), kind=kOutput, calls=%fused_computation.161 | convolution fusion | flops 2415919104 | bytes 10616832 | tf_op jit(solution)/shard_map/dot_general | solution.py:117
  217.9 2.4 all-gather.5.cloned.1.call-done
  220.3 10.8 %convert_reduce_fusion.4 = (f32[768]{0:T(1024)}, bf16[2048,768]{1,0:T(8,128)(2,1)S(1)}, bf16[2048,768]{1,0:T(8,128)(2,1)}) fusion(f32[2048,768]{1,0:T(8,128)} %fusion.111, f32[768]{0:T(1024)} %param.45, bf16[2048,768]{1,0:T(8,128)(2,1)} %param.26, bf16[768,768]{0,1:T(8,128)(2,1)} %all-gather.5.cloned.1.call-done), kind=kOutput, calls=%fused_computation.46 | convolution fusion | flops 2455239936 | bytes 16914432 | tf_op jit(solution)/shard_map/td,fd->tf/dot_general | solution.py:125
  231.1 1.7 copy-done.57
  232.8 4.0 convolution_convert_fusion
  238.7 6.6 convolution_convert_fusion.1
  245.2 58.7 %all-reduce.8.cloned.1.call-done = bf16[2048,768]{1,0:T(8,128)(2,1)} async-done(((bf16[2048,768]{1,0:T(8,128)(2,1)}), bf16[2048,768]{1,0:T(8,128)(2,1)}) %all-reduce.8.cloned.1.call-update) | async-done | bytes 3145744 | tf_op jit(solution)/shard_map/psum | solution.py:130
  303.9 7.1 %fusion.30 = (f32[768]{0:T(1024)}, f32[2048]{0:T(1024)S(1)}, f32[2048]{0:T(1024)S(1)}, f32[768]{0:T(1024)}) fusion(bf16[2048,768]{1,0:T(8,128)(2,1)} %all-reduce.8.cloned.1.call-done, f32[2048]{0:T(1024)} %copy-done.27, f32[2048]{0:T(1024)S(1)} %broadcast_multiply_fusion.4, f32[768]{0:T(1024)S(1)} %get-tuple-element.131, ...), kind=kLoop, calls=%fused_computation.43 | loop fusion | flops 22014464 | bytes 9482240 | tf_op jit(solution)/shard_map/reduce_sum | solution.py:167
  311.1 4.7 fusion.106
  315.8 2.7 copy-done.3
  318.5 2.3 fusion.78
  320.7 4.9 convolution_convert_fusion.3
  325.6 3.4 reshape.146
  329.0 3.6 copy.128
  332.7 5.1 fusion.81
  337.8 10.3 %fusion.71 = bf16[32,64,3,64]{1,3,2,0:T(8,128)(2,1)} fusion(f32[32,3,64,64]{2,3,1,0:T(8,128)} %fusion.81, f32[32,3,64,64]{2,3,1,0:T(8,128)} %copy-done.4, f32[32,3,64]{2,1,0:T(4,128)S(1)} %copy-done.23, f32[32,64,3,64]{1,0,3,2:T(8,128)} %squeeze.10, f32[3,64]{1,0:T(4,128)S(1)} %copy-done.47), kind=kOutput, calls=%fused_computation.91 | convolution fusion | flops 54270016 | bytes 5530368 | tf_op jit(solution)/shard_map/rhqk,rqhd->rkhd/dot_general | solution.py:150
  348.1 8.1 %convert_reduce_fusion.6 = (f32[3,64]{1,0:T(4,128)S(1)}, bf16[32,64,3,64]{3,1,2,0:T(8,128)(2,1)}) fusion(bf16[32,64,3,64]{3,1,2,0:T(8,128)(2,1)} %copy.123, f32[32,3,64,64]{2,3,1,0:T(8,128)} %fusion.81, f32[32,3,64,64]{2,3,1,0:T(8,128)} %copy-done.4, f32[32,3,64]{2,1,0:T(4,128)S(1)} %copy-done.23), kind=kOutput, calls=%fused_computation.60 | convolution fusion | flops 54269824 | bytes 4743936 | tf_op jit(solution)/shard_map/rhqk,rkhd->rqhd/dot_general | solution.py:147
  356.2 4.4 convert_reduce_fusion.5
  360.6 3.6 copy.131
  364.2 3.5 stack.42
  367.8 2.1 constant_dynamic-update-slice_fusion.2
  369.9 3.6 copy.133
  373.4 3.5 stack.43
  377.0 3.2 copy.135
  380.1 3.5 stack.44
  383.7 2.2 constant_dynamic-update-slice_fusion.1
  385.8 2.1 constant_dynamic-update-slice_fusion
  387.9 6.0 bitcast_convert_fusion
  394.0 7.1 %fusion.112 = f32[768,768]{1,0:T(8,128)} fusion(bf16[2048,768]{1,0:T(8,128)(2,1)} %add_convert_fusion.1, bf16[2048,768]{1,0:T(8,128)(2,1)} %copy-done.57), kind=kOutput, calls=%fused_computation.162 | convolution fusion | flops 2415919104 | bytes 8650752 | tf_op jit(solution)/shard_map/td,tf->df/dot_general | solution.py:127
  401.4 6.9 fusion.113
  408.4 5.2 fusion.65
  413.6 4.2 copy.149
  417.8 4.7 reshape.151
  423.4 1.8 copy.137
  425.3 1.8 copy.138
  429.0 85.0 %all-reduce.10.cloned.1.call-done = (bf16[2048,768]{1,0:T(8,128)(2,1)}, bf16[2048,768]{1,0:T(8,128)(2,1)}) async-done(((bf16[2048,768]{1,0:T(8,128)(2,1)}, bf16[2048,768]{1,0:T(8,128)(2,1)}), (bf16[2048,768]{1,0:T(8,128)(2,1)}, bf16[2048,768]{1,0:T(8,128)(2,1)})) %all-reduce.10.cloned.1.call-update) | async-done | bytes 6291472 | tf_op jit(solution)/shard_map/psum | solution.py:121
  514.0 5.2 fusion.31
  519.3 37.8 %all-reduce = (f32[6,768]{1,0:T(8,128)S(1)}, f32[2,192]{1,0:T(2,128)S(1)}, f32[768]{0:T(1024)S(1)}) all-reduce(f32[6,768]{1,0:T(8,128)S(1)} %stack.52, f32[2,192]{1,0:T(2,128)S(1)} %pad_maximum_fusion, f32[768]{0:T(1024)S(1)} %copy-done.53), channel_id=1, replica_groups=mesh['dp'=8,'mp'=4] {'dp'}, use_global_device_ids=true, to_apply=%region_29.30 | all-reduce | flops 5760 | bytes 46080 | tf_op jit(solution)/shard_map/psum | solution.py:179
  562.6 5.0 reduce-scatter.11.cloned.1.call-done
  569.8 67.9 %reduce-scatter.13.cloned.1.call-done = f32[96,576]{1,0:T(8,128)} async-done(((f32[768,576]{1,0:T(8,128)}), f32[96,576]{1,0:T(8,128)}) %reduce-scatter.13.cloned.1.call-update) | async-done | bytes 221200
  637.7 1.9 reshape.152
  645.3 6.1 psum.70
  651.4 10.5 %fusion.16 = (bf16[2048,768]{1,0:T(8,128)(2,1)}, bf16[2048,768]{1,0:T(8,128)(2,1)}) fusion(f32[2048,768]{1,0:T(8,128)} %copy-done.3, bf16[2048,768]{1,0:T(8,128)(2,1)S(1)} %copy-done, bf16[2048,768]{1,0:T(8,128)(2,1)} %get-tuple-element.140, f32[2048]{0:T(1024)} %broadcast_multiply_fusion, f32[2048]{0:T(1024)} %broadcast_multiply_fusion.1, ...), kind=kLoop, calls=%fused_computation.29 | loop fusion | flops 28311552 | bytes 25207808 | tf_op jit(solution)/shard_map/convert_element_type | solution.py:162
  662.1 19.7 %psum.71 = f32[]{:T(128)} all-reduce(f32[]{:T(128)} %psum.70), channel_id=1, replica_groups=mesh['dp'=8,'mp'=4] {'dp'}, use_global_device_ids=true, to_apply=%region_39.40 | all-reduce | flops 1 | bytes 8 | tf_op jit(solution)/shard_map/psum | solution.py:188
  (186 shorter events, 37.1 us)
Async XLA Ops:
  8.0 2.8 copy-start
  8.0 3.9 copy-start.31
  8.0 4.5 copy-start.13
  8.1 193.7 %all-reduce.6.cloned.1.call-start = ((), (), s32[]{:S(2)}) async-start(), calls=%async_computation.4 | async-start | bytes 6291456 | tf_op jit(solution)/shard_map/psum | solution.py:113
  10.9 45.8 %copy-start.25 = (f32[2048]{0:T(1024)}, f32[2048]{0:T(1024)S(1)}, u32[]{:S(2)}) copy-start(f32[2048]{0:T(1024)S(1)} %broadcast_multiply_fusion.5) | copy-start | bytes 24580
  12.0 48.1 %copy-start.32 = (f32[2048]{0:T(1024)}, f32[2048]{0:T(1024)S(1)}, u32[]{:S(2)}) copy-start(f32[2048]{0:T(1024)S(1)} %add_rsqrt_fusion.1) | copy-start | bytes 24580
  12.6 47.5 %copy-start.35 = (f32[768]{0:T(1024)}, f32[768]{0:T(1024)S(1)}, u32[]{:S(2)}) copy-start(f32[768]{0:T(1024)S(1)} %get-tuple-element.133) | copy-start | bytes 9220
  12.6 47.5 %copy-start.54 = (f32[768]{0:T(1024)}, f32[768]{0:T(1024)S(1)}, u32[]{:S(2)}) copy-start(f32[768]{0:T(1024)S(1)} %get-tuple-element.132) | copy-start | bytes 9220
  61.1 2.0 copy-start.50
  61.1 2.2 copy-start.17
  61.1 2.9 copy-start.34
  63.2 58.3 %copy-start.44 = (f32[3,64]{1,0:T(4,128)}, f32[3,64]{1,0:T(4,128)S(1)}, u32[]{:S(2)}) copy-start(f32[3,64]{1,0:T(4,128)S(1)} %add.266) | copy-start | bytes 2308
  63.3 51.6 %copy-start.46 = (f32[3,64]{1,0:T(4,128)}, f32[3,64]{1,0:T(4,128)S(1)}, u32[]{:S(2)}) copy-start(f32[3,64]{1,0:T(4,128)S(1)} %add.269) | copy-start | bytes 2308
  120.6 4.1 copy-start.4
  120.6 4.1 copy-start.16
  120.6 3.0 copy-start.5
  134.3 76.0 %all-gather.3.cloned.1.call-start = ((), (), s32[]{:S(2)}) async-start(), calls=%async_computation.5 | async-start | bytes 1327104 | tf_op jit(solution)/shard_map/all_gather | solution.py:80
  136.0 84.2 %all-gather.5.cloned.1.call-start = ((), (), s32[]{:S(2)}) async-start(), calls=%async_computation.6 | async-start | bytes 1327104 | tf_op jit(solution)/shard_map/all_gather | solution.py:81
  137.8 166.2 %all-reduce.8.cloned.1.call-start = ((), (), s32[]{:S(2)}) async-start(), calls=%async_computation.7 | async-start | bytes 6291456 | tf_op jit(solution)/shard_map/psum | solution.py:130
  201.8 3.2 copy-start.1
  205.0 2.4 copy-start.37
  220.3 12.5 %copy-start.56 = (bf16[768,768]{1,0:T(8,128)(2,1)S(1)}, bf16[768,768]{1,0:T(8,128)(2,1)}, u32[]{:S(2)}) copy-start(bf16[768,768]{1,0:T(8,128)(2,1)} %all-gather.3.cloned.1.call-done) | copy-start | bytes 3538948
  236.9 190.5 %reduce-scatter.15.cloned.1.call-start = ((), (), s32[]{:S(2)}) async-start(), calls=%async_computation.11 | async-start | bytes 884736
  303.9 7.1 %copy-start.2 = (bf16[2048,768]{1,0:T(8,128)(2,1)S(1)}, bf16[2048,768]{1,0:T(8,128)(2,1)}, u32[]{:S(2)}) copy-start(bf16[2048,768]{1,0:T(8,128)(2,1)} %all-reduce.6.cloned.1.call-done) | copy-start | bytes 9437188
  303.9 7.1 %copy-start.6 = (bf16[2048,768]{1,0:T(8,128)(2,1)S(1)}, bf16[2048,768]{1,0:T(8,128)(2,1)}, u32[]{:S(2)}) copy-start(bf16[2048,768]{1,0:T(8,128)(2,1)} %all-reduce.8.cloned.1.call-done) | copy-start | bytes 9437188
  303.9 7.1 %copy-start.8 = (bf16[2048,768]{1,0:T(8,128)(2,1)S(1)}, bf16[2048,768]{1,0:T(8,128)(2,1)}, u32[]{:S(2)}) copy-start(bf16[2048,768]{1,0:T(8,128)(2,1)} %param.26) | copy-start | bytes 9437188
  303.9 7.1 %copy-start.28 = (f32[2048]{0:T(1024)S(1)}, f32[2048]{0:T(1024)}, u32[]{:S(2)}) copy-start(f32[2048]{0:T(1024)} %copy-done.27) | copy-start | bytes 24580
  311.0 7.4 %copy-start.7 = (bf16[2048,192]{0,1:T(8,128)(2,1)S(1)}, bf16[2048,192]{0,1:T(8,128)(2,1)}, u32[]{:S(2)}) copy-start(bf16[2048,192]{0,1:T(8,128)(2,1)} %reshape.145) | copy-start | bytes 2359300
  315.8 2.7 copy-start.3
  325.6 7.0 copy-start.45
  332.6 5.1 copy-start.23
  332.6 5.1 copy-start.47
  360.5 153.4 %all-reduce.10.cloned.1.call-start = ((), (), s32[]{:S(2)}) async-start(), calls=%async_computation.12 | async-start | bytes 12582912 | tf_op jit(solution)/shard_map/psum | solution.py:121
  383.7 4.3 copy-start.15
  394.0 167.0 %reduce-scatter.9.cloned.1.call-start = ((), (), s32[]{:S(2)}) async-start(), calls=%async_computation.8 | async-start | bytes 2654208 | tf_op jit(solution)/shard_map/reduce_scatter | solution.py:176
  401.1 7.3 %copy-start.26 = (f32[2048]{0:T(1024)S(1)}, f32[2048]{0:T(1024)}, u32[]{:S(2)}) copy-start(f32[2048]{0:T(1024)} %copy-done.25) | copy-start | bytes 24580
  401.1 7.3 %copy-start.33 = (f32[2048]{0:T(1024)S(1)}, f32[2048]{0:T(1024)}, u32[]{:S(2)}) copy-start(f32[2048]{0:T(1024)} %copy-done.32) | copy-start | bytes 24580
  401.1 7.3 %copy-start.36 = (f32[768]{0:T(1024)S(1)}, f32[768]{0:T(1024)}, u32[]{:S(2)}) copy-start(f32[768]{0:T(1024)} %copy-done.35) | copy-start | bytes 9220
  401.1 7.3 %copy-start.55 = (f32[768]{0:T(1024)S(1)}, f32[768]{0:T(1024)}, u32[]{:S(2)}) copy-start(f32[768]{0:T(1024)} %copy-done.54) | copy-start | bytes 9220
  401.1 166.4 %reduce-scatter.11.cloned.1.call-start = ((), (), s32[]{:S(2)}) async-start(), calls=%async_computation.9 | async-start | bytes 2654208 | tf_op jit(solution)/shard_map/reduce_scatter | solution.py:177
  408.3 229.3 %reduce-scatter.13.cloned.1.call-start = ((), (), s32[]{:S(2)}) async-start(), calls=%async_computation.10 | async-start | bytes 2211840
  417.8 4.8 copy-start.14
  422.5 4.6 copy-start.39
  422.5 4.6 copy-start.38
  422.5 4.6 copy-start.43
  422.5 4.6 copy-start.42
  514.0 5.3 copy-start.53
  557.1 82.4 %copy-start.30 = (f32[6,768]{1,0:T(8,128)}, f32[6,768]{1,0:T(8,128)S(1)}, u32[]{:S(2)}) copy-start(f32[6,768]{1,0:T(8,128)S(1)} %get-tuple-element.136) | copy-start | bytes 55300
  557.1 82.4 %copy-start.40 = (f32[768]{0:T(1024)}, f32[768]{0:T(1024)S(1)}, u32[]{:S(2)}) copy-start(f32[768]{0:T(1024)S(1)} %get-tuple-element.138) | copy-start | bytes 9220
  557.1 82.4 %copy-start.48 = (f32[2,192]{1,0:T(2,128)}, f32[2,192]{1,0:T(2,128)S(1)}, u32[]{:S(2)}) copy-start(f32[2,192]{1,0:T(2,128)S(1)} %get-tuple-element.137) | copy-start | bytes 4612
  661.9 24.6 %copy-start.49 = (f32[2,192]{1,0:T(2,128)S(1)}, f32[2,192]{1,0:T(2,128)}, u32[]{:S(2)}) copy-start(f32[2,192]{1,0:T(2,128)} %copy-done.48) | copy-start | bytes 4612
  661.9 24.6 %copy-start.51 = (f32[2,192]{1,0:T(2,128)S(1)}, f32[2,192]{1,0:T(2,128)}, u32[]{:S(2)}) copy-start(f32[2,192]{1,0:T(2,128)} %param.42) | copy-start | bytes 4612
  662.0 25.9 %copy-start.41 = (f32[768]{0:T(1024)S(1)}, f32[768]{0:T(1024)}, u32[]{:S(2)}) copy-start(f32[768]{0:T(1024)} %copy-done.40) | copy-start | bytes 9220
  662.0 25.9 %copy-start.52 = (f32[768]{0:T(1024)S(1)}, f32[768]{0:T(1024)}, u32[]{:S(2)}) copy-start(f32[768]{0:T(1024)} %param.45) | copy-start | bytes 9220
  662.0 28.7 %copy-start.18 = (f32[192,96]{1,0:T(8,128)S(1)}, f32[192,96]{1,0:T(8,128)}, u32[]{:S(2)}) copy-start(f32[192,96]{1,0:T(8,128)} %param.30) | copy-start | bytes 221188
  662.0 28.6 %copy-start.29 = (f32[192,96]{1,0:T(8,128)S(1)}, f32[192,96]{1,0:T(8,128)}, u32[]{:S(2)}) copy-start(f32[192,96]{1,0:T(8,128)} %param.32) | copy-start | bytes 221188
  662.0 30.3 %copy-start.9 = (f32[96,768]{1,0:T(8,128)S(1)}, f32[96,768]{1,0:T(8,128)}, u32[]{:S(2)}) copy-start(f32[96,768]{1,0:T(8,128)} %param.33) | copy-start | bytes 884740
  662.0 30.3 %copy-start.11 = (f32[96,768]{1,0:T(8,128)S(1)}, f32[96,768]{1,0:T(8,128)}, u32[]{:S(2)}) copy-start(f32[96,768]{1,0:T(8,128)} %reduce-scatter.9.cloned.1.call-done) | copy-start | bytes 884740
  662.0 30.3 %copy-start.19 = (f32[96,768]{1,0:T(8,128)S(1)}, f32[96,768]{1,0:T(8,128)}, u32[]{:S(2)}) copy-start(f32[96,768]{1,0:T(8,128)} %param.35) | copy-start | bytes 884740
  662.0 30.3 %copy-start.20 = (f32[96,768]{1,0:T(8,128)S(1)}, f32[96,768]{1,0:T(8,128)}, u32[]{:S(2)}) copy-start(f32[96,768]{1,0:T(8,128)} %param.34) | copy-start | bytes 884740
  682.5 10.9 %copy-start.10 = (f32[768,96]{0,1:T(8,128)S(1)}, f32[768,96]{0,1:T(8,128)}, u32[]{:S(2)}) copy-start(f32[768,96]{0,1:T(8,128)} %param.36) | copy-start | bytes 884740
  682.5 10.9 %copy-start.12 = (f32[768,96]{0,1:T(8,128)S(1)}, f32[768,96]{0,1:T(8,128)}, u32[]{:S(2)}) copy-start(f32[768,96]{0,1:T(8,128)} %reduce-scatter.11.cloned.1.call-done) | copy-start | bytes 884740
  682.5 10.9 %copy-start.21 = (f32[768,96]{0,1:T(8,128)S(1)}, f32[768,96]{0,1:T(8,128)}, u32[]{:S(2)}) copy-start(f32[768,96]{0,1:T(8,128)} %param.38) | copy-start | bytes 884740
  683.9 9.4 %copy-start.22 = (f32[768,96]{0,1:T(8,128)S(1)}, f32[768,96]{0,1:T(8,128)}, u32[]{:S(2)}) copy-start(f32[768,96]{0,1:T(8,128)} %param.37) | copy-start | bytes 884740
  (3 other events, 3.3 us)
Sparse Core Ops, SparseCore 0:
  134.4 67.2 all-reduce.5
  237.0 66.9 all-reduce.7
  394.1 119.8 all-reduce.9
Sparse Core Ops, SparseCore 1:
  137.6 40.2 all-gather.2
  180.5 39.8 all-gather.4
  360.6 62.6 reduce-scatter.14
  427.2 68.3 reduce-scatter.8
  499.5 68.0 reduce-scatter.10
  571.5 66.1 reduce-scatter.12
